TPU v7x, 512 devices: a whole 4x8x8 slice. The times are simulated.
512 devices in a mesh: row: 32 (over y, x), col: 16 (over z, core).
Axes of the slice: x: 4, y: 8, z: 8, core: 2. Of those that a mesh axis runs over, the one named last changes fastest.
Arguments:
- gram_panel: float32 [8192, 1024], P('row', 'col'), may hold values from -2973.8 to 2973.8, as said below
- left_factor: bfloat16 [8192, 16384], P('row', 'col'), may hold values from -0.42426407 to 0.42426407
- solved_prev: bfloat16 [16384, 8192], P('row', 'col'), may hold values from -0.59765625 to 0.59765625
- right_block: float32 [1024, 8192], P('row', 'col'), may hold values from -6 to 6
Outputs:
- panel_factor: float32 [8192, 1024], P('row', 'col')
- solved_panel: float32 [1024, 8192], P('row', 'col')
Inputs may be any that keep to these rules, and one draw needn't show every extreme that they name: The rows of gram_panel at the panel's indices minus the product of the corresponding rows of left_factor with their transpose form a symmetric positive definite matrix.
All inputs are finite; a program needn't handle non-finite values.
Results may differ from a plain program's by a relative error of at most 0.0006.
Values may be sent and summed in bfloat16 or wider, within the bound.
No kernel may reach another device: no remote copies, remote signals or barrier semaphores. Data moves between devices by JAX's collectives and lax.ppermute only.
A program may use at most 64 MiB of HBM per device.

v0:
```python
import jax
import jax.numpy as jnp
from jax import lax
from jax.sharding import PartitionSpec as P


def spread(value, axis, source):
    kept = jnp.where(lax.axis_index(axis) == source, value, 0).astype(value.dtype)
    return lax.psum(kept, axis)


def invert(diagonal):
    factor = jnp.linalg.cholesky(diagonal)
    identity = jnp.eye(diagonal.shape[0], dtype=jnp.float32)
    return jax.scipy.linalg.solve_triangular(factor, identity, lower=True)


def body(gram_panel, left_factor, solved_prev, right_block):
    row_count = lax.axis_size("row")
    col_count = lax.axis_size("col")
    row_place = lax.axis_index("row")
    col_place = lax.axis_index("col")
    block_rows = right_block.shape[0]
    col_width = gram_panel.shape[1]
    per_column = row_count // col_count
    strip_width = left_factor.shape[1] // per_column
    chosen = lax.all_gather(left_factor[:block_rows], "row", axis=0, tiled=True)
    portion = chosen
    summed = lax.psum_scatter(
        jnp.einsum("pk,mk->pm", portion, left_factor, preferred_element_type=jnp.float32),
        "col",
        scatter_dimension=0,
        tiled=True,
    )
    update = gram_panel - summed.T
    diag_part = lax.all_gather(update[:block_rows], "row", axis=0, tiled=True)
    diagonal = lax.all_gather(diag_part, "col", axis=1, tiled=True)
    inverse = invert(diagonal)
    inverse_cols = lax.dynamic_slice_in_dim(inverse, col_place * col_width, col_width, 0)
    inverse_part = inverse_cols
    panel_factor = lax.dot_general(
        lax.all_gather(update, "col", axis=1, tiled=True),
        inverse_part,
        (((1,), (1,)), ((), ())),
        precision=lax.Precision.HIGHEST,
    )
    strip_piece = lax.dynamic_slice_in_dim(
        chosen, row_place % per_column * strip_width, strip_width, 1
    )
    strip_piece = spread(strip_piece, "col", row_place // per_column)
    portion = strip_piece
    reduced = right_block - lax.psum_scatter(
        jnp.dot(portion, solved_prev, preferred_element_type=jnp.float32),
        "row",
        scatter_dimension=0,
        tiled=True,
    )
    inverse_rows = lax.dynamic_slice_in_dim(inverse, row_place * block_rows, block_rows, 0)
    inverse_part = inverse_rows
    solved_panel = jnp.dot(
        inverse_part,
        lax.all_gather(reduced, "row", axis=0, tiled=True),
        precision=lax.Precision.HIGHEST,
    )
    return (panel_factor, solved_panel)


def solution(mesh):
    in_specs = (P("row", "col"), P("row", "col"), P("row", "col"), P("row", "col"))
    out_specs = (P("row", "col"), P("row", "col"))
    return jax.shard_map(body, mesh=mesh, in_specs=in_specs, out_specs=out_specs, check_vma=False)
```

profile of v0, /device:TPU:1, one launch (start us, length us, event | category | flops | bytes accessed | tf_op | source)
XLA Modules:
  0.0 915.5 jit_solution(4656776217967420164)
XLA Ops:
  8.8 87.9 %all-gather.5.cloned.1.call-done = bf16[1024,1024]{1,0:T(8,128)(2,1)} async-done(((bf16[32,1024]{1,0:T(8,128)(2,1)}), bf16[1024,1024]{1,0:T(8,128)(2,1)}) %all-gather.5.cloned.1.call-update) | async-done | bytes 2097168 | tf_op jit(solution)/shard_map/all_gather | solution.py:27
  96.8 2.4 dynamic-slice_select_fusion
  99.2 3.4 fusion.77
  102.7 115.2 %all-reduce.3.cloned.1.call-done = bf16[1024,512]{1,0:T(8,128)(2,1)} async-done(((bf16[1024,512]{1,0:T(8,128)(2,1)}), bf16[1024,512]{1,0:T(8,128)(2,1)}) %all-reduce.3.cloned.1.call-update) | async-done | bytes 1048592 | tf_op jit(solution)/shard_map/psum | solution.py:9
  218.0 3.3 fusion.78
  221.3 57.3 %reduce-scatter.3.cloned.1.call-done = f32[64,256]{1,0:T(8,128)} async-done(((f32[1024,256]{1,0:T(8,128)}), f32[64,256]{1,0:T(8,128)}) %reduce-scatter.3.cloned.1.call-update) | async-done | bytes 65552 | tf_op jit(solution)/shard_map/reduce_scatter | solution.py:29
  279.6 38.7 %all_gather.17 = f32[1024,64]{1,0:T(8,128)S(1)} all-gather(f32[32,64]{1,0:T(8,128)S(1)} %copy.7), channel_id=1, replica_groups=mesh['row'=32,'col'=16] {'row'}, dimensions={0}, use_global_device_ids=true | all-gather | bytes 270336 | tf_op jit(solution)/shard_map/all_gather | solution.py:36
  319.3 180.5 %reduce-scatter.5.cloned.1.call-done = f32[32,512]{1,0:T(8,128)} async-done(((f32[1024,512]{1,0:T(8,128)}), f32[32,512]{1,0:T(8,128)}) %reduce-scatter.5.cloned.1.call-update) | async-done | bytes 65552 | tf_op jit(solution)/shard_map/reduce_scatter | solution.py:52
  501.7 2.4 fusion.21
  504.2 47.7 %all-gather.9.cloned.1.call-done = f32[1024,1024]{0,1:T(8,128)} async-done(((f32[1024,64]{0,1:T(8,128)}), f32[1024,1024]{0,1:T(8,128)}) %all-gather.9.cloned.1.call-update) | async-done | bytes 4194320 | tf_op jit(solution)/shard_map/all_gather | solution.py:37
  551.8 5.8 copy.9
  557.7 4.4 fusion
  564.1 11.7 %cholesky.223 = f32[128,128]{1,0:T(8,128)S(1)} custom-call(f32[128,128]{1,0:T(8,128)S(1)} %cholesky.580), custom_call_target="Cholesky" | custom-call | tf_op jit(solution)/shard_map/jit(cholesky)/cholesky | solution.py:13
  575.9 9.8 %custom-call.63 = f32[1,128,128]{1,2,0:T(8,128)S(1)} custom-call(f32[1,128,128]{2,1,0:T(8,128)S(1)} %get-tuple-element.66), custom_call_target="InvertDiagBlocksLowerTriangular" | custom-call | tf_op jit(solution)/shard_map/jit(cholesky)/cholesky | solution.py:13
  585.7 2.5 cholesky.255
  588.2 2.3 constant_dynamic-update-slice_fusion.29
  592.1 11.9 %cholesky.244 = f32[128,128]{1,0:T(8,128)S(1)} custom-call(f32[128,128]{1,0:T(8,128)S(1)} %cholesky.584), custom_call_target="Cholesky" | custom-call | tf_op jit(solution)/shard_map/jit(cholesky)/cholesky | solution.py:13
  604.6 9.8 %custom-call.64 = f32[1,128,128]{1,2,0:T(8,128)S(1)} custom-call(f32[1,128,128]{2,1,0:T(8,128)S(1)} %get-tuple-element.63), custom_call_target="InvertDiagBlocksLowerTriangular" | custom-call | tf_op jit(solution)/shard_map/jit(cholesky)/cholesky | solution.py:13
  617.8 11.7 %cholesky.468 = f32[128,128]{1,0:T(8,128)S(1)} custom-call(f32[128,128]{1,0:T(8,128)S(1)} %cholesky.589), custom_call_target="Cholesky" | custom-call | tf_op jit(solution)/shard_map/jit(cholesky)/cholesky | solution.py:13
  630.8 9.8 %custom-call.65 = f32[1,128,128]{1,2,0:T(8,128)S(1)} custom-call(f32[1,128,128]{2,1,0:T(8,128)S(1)} %get-tuple-element.60), custom_call_target="InvertDiagBlocksLowerTriangular" | custom-call | tf_op jit(solution)/shard_map/jit(cholesky)/cholesky | solution.py:13
  641.8 2.3 convolution_subtract_fusion.7
  644.2 11.9 %cholesky.487 = f32[128,128]{1,0:T(8,128)S(1)} custom-call(f32[128,128]{1,0:T(8,128)S(1)} %cholesky.594), custom_call_target="Cholesky" | custom-call | tf_op jit(solution)/shard_map/jit(cholesky)/cholesky | solution.py:13
  657.3 9.8 %custom-call.66 = f32[1,128,128]{1,2,0:T(8,128)S(1)} custom-call(f32[1,128,128]{2,1,0:T(8,128)S(1)} %get-tuple-element.57), custom_call_target="InvertDiagBlocksLowerTriangular" | custom-call | tf_op jit(solution)/shard_map/jit(cholesky)/cholesky | solution.py:13
  668.2 2.4 convolution_subtract_fusion.8
  670.6 11.7 %cholesky.506 = f32[128,128]{1,0:T(8,128)S(1)} custom-call(f32[128,128]{1,0:T(8,128)S(1)} %cholesky.599), custom_call_target="Cholesky" | custom-call | tf_op jit(solution)/shard_map/jit(cholesky)/cholesky | solution.py:13
  683.6 10.2 %custom-call.67 = f32[1,128,128]{1,2,0:T(8,128)S(1)} custom-call(f32[1,128,128]{2,1,0:T(8,128)S(1)} %get-tuple-element.54), custom_call_target="InvertDiagBlocksLowerTriangular" | custom-call | tf_op jit(solution)/shard_map/jit(cholesky)/cholesky | solution.py:13
  694.8 2.3 convolution_subtract_fusion.9
  697.1 11.7 %cholesky.526 = f32[128,128]{1,0:T(8,128)S(1)} custom-call(f32[128,128]{1,0:T(8,128)S(1)} %cholesky.604), custom_call_target="Cholesky" | custom-call | tf_op jit(solution)/shard_map/jit(cholesky)/cholesky | solution.py:13
  710.2 9.8 %custom-call.68 = f32[1,128,128]{1,2,0:T(8,128)S(1)} custom-call(f32[1,128,128]{2,1,0:T(8,128)S(1)} %get-tuple-element.51), custom_call_target="InvertDiagBlocksLowerTriangular" | custom-call | tf_op jit(solution)/shard_map/jit(cholesky)/cholesky | solution.py:13
  723.0 11.9 %cholesky.546 = f32[128,128]{1,0:T(8,128)S(1)} custom-call(f32[128,128]{1,0:T(8,128)S(1)} %cholesky.609), custom_call_target="Cholesky" | custom-call | tf_op jit(solution)/shard_map/jit(cholesky)/cholesky | solution.py:13
  736.2 9.8 %custom-call.69 = f32[1,128,128]{1,2,0:T(8,128)S(1)} custom-call(f32[1,128,128]{2,1,0:T(8,128)S(1)} %get-tuple-element.48), custom_call_target="InvertDiagBlocksLowerTriangular" | custom-call | tf_op jit(solution)/shard_map/jit(cholesky)/cholesky | solution.py:13
  748.7 11.7 %cholesky.564 = f32[128,128]{1,0:T(8,128)S(1)} custom-call(f32[128,128]{1,0:T(8,128)S(1)} %convolution_subtract_fusion.11), custom_call_target="Cholesky" | custom-call | tf_op jit(solution)/shard_map/jit(cholesky)/cholesky | solution.py:13
  767.4 4.8 select_select_fusion
  772.3 22.5 %while.1 = (s32[]{:T(128)}, f32[1024,1024]{1,0:T(8,128)}, s32[8,2]{0,1:T(2,128)S(1)}, f32[8,128,128]{2,1,0:T(8,128)S(1)}, s32[]{:T(128)}) while((s32[]{:T(128)}, f32[1024,1024]{1,0:T(8,128)}, s32[8,2]{0,1:T(2,128)S(1)}, f32[8,128,128]{2,1,0:T(8,128)S(1)}, s32[]{:T(128)}) %tuple.61), condition=%wide.while_cond, body=%wide.while_body.sunk | while | flops 2 | bytes 131181 | solution.py:15
  772.9 2.2 bitcast_dynamic-update-slice_fusion.2
  775.7 2.2 bitcast_dynamic-update-slice_fusion.2
  778.5 2.2 bitcast_dynamic-update-slice_fusion.2
  781.3 2.2 bitcast_dynamic-update-slice_fusion.2
  784.2 2.2 bitcast_dynamic-update-slice_fusion.2
  787.0 2.2 bitcast_dynamic-update-slice_fusion.2
  789.8 2.2 bitcast_dynamic-update-slice_fusion.2
  794.7 78.8 %custom-call.70 = f32[8,128,128]{1,2,0:T(8,128)S(1)} custom-call(f32[8,128,128]{2,1,0:T(8,128)S(1)} %get-tuple-element.9), custom_call_target="InvertDiagBlocksLowerTriangular" | custom-call | tf_op jit(solution)/shard_map/jit(_solve_triangular)/triangular_solve | solution.py:15
  885.0 2.2 fusion.18
  888.8 2.6 convolution_subtract_fusion.2
  892.9 2.8 convolution_subtract_fusion.1
  897.2 3.5 convolution_subtract_fusion.3
  902.2 3.6 fusion.53
  905.7 2.6 fusion.45
  (98 shorter events, 54.9 us)
Async XLA Ops:
  7.2 210.8 %copy-start = (bf16[512,512]{1,0:T(8,128)(2,1)S(1)}, bf16[512,512]{1,0:T(8,128)(2,1)}, u32[]{:S(2)}) copy-start(bf16[512,512]{1,0:T(8,128)(2,1)} %param.6) | copy-start | bytes 1572868
  7.2 89.6 %all-gather.5.cloned.1.call-start = ((), (), s32[]{:S(2)}) async-start(), calls=%async_computation.2 | async-start | bytes 2162688 | tf_op jit(solution)/shard_map/all_gather | solution.py:27
  8.8 209.2 %all-reduce.3.cloned.1.call-start = ((), (), s32[]{:S(2)}) async-start(), calls=%async_computation.6 | async-start | bytes 2097152 | tf_op jit(solution)/shard_map/psum | solution.py:9
  99.2 179.5 %reduce-scatter.3.cloned.1.call-start = ((), (), s32[]{:S(2)}) async-start(), calls=%async_computation.3 | async-start | bytes 1114112 | tf_op jit(solution)/shard_map/reduce_scatter | solution.py:29
  102.6 176.0 %copy-start.4 = (f32[256,64]{0,1:T(8,128)S(1)}, f32[256,64]{0,1:T(8,128)}, u32[]{:S(2)}) copy-start(f32[256,64]{0,1:T(8,128)} %param.4) | copy-start | bytes 196612
  102.7 397.2 %copy-start.5 = (f32[32,512]{1,0:T(8,128)S(1)}, f32[32,512]{1,0:T(8,128)}, u32[]{:S(2)}) copy-start(f32[32,512]{1,0:T(8,128)} %param.7) | copy-start | bytes 196612
  102.7 397.1 %reduce-scatter.5.cloned.1.call-start = ((), (), s32[]{:S(2)}) async-start(), calls=%async_computation.7 | async-start | bytes 2162688 | tf_op jit(solution)/shard_map/reduce_scatter | solution.py:52
  221.3 330.6 %all-gather.9.cloned.1.call-start = ((), (), s32[]{:S(2)}) async-start(), calls=%async_computation.5 | async-start | bytes 4456448 | tf_op jit(solution)/shard_map/all_gather | solution.py:37
  279.5 224.6 %copy-start.3 = (f32[256,64]{0,1:T(8,128)}, f32[256,64]{0,1:T(8,128)S(1)}, u32[]{:S(2)}) copy-start(f32[256,64]{0,1:T(8,128)S(1)} %bitcast_subtract_fusion) | copy-start | bytes 196612
  319.2 582.9 %all-gather.11.cloned.1.call-start = ((), (), s32[]{:S(2)}) async-start(), calls=%async_computation.8 | async-start | bytes 2162688 | tf_op jit(solution)/shard_map/all_gather | solution.py:62
  501.3 404.4 %all-gather.7.cloned.1.call-start = ((), (), s32[]{:S(2)}) async-start(), calls=%async_computation.4 | async-start | bytes 1114112 | tf_op jit(solution)/shard_map/all_gather | solution.py:42
  562.1 2.0 copy-start.2
  873.6 4.7 copy-start.1
Sparse Core Ops, SparseCore 0:
  11.8 84.9 all-gather.4
  99.3 118.6 all-reduce.2
  221.0 57.5 reduce-scatter.2
  282.9 216.8 reduce-scatter.4
  502.0 49.8 all-gather.8
  555.9 77.5 all-gather.10
  636.4 43.9 all-gather.6
where the time goes:
time: 920 us; the launch traced here: 915 us
  waiting for transfers between devices  489 us (53%)
  other arithmetic  268 us (29%)
  matrix products  64.5 us (7%)
  blocking collectives  38.7 us (4%)
  local copies, waits for them, and re-layouts  35.2 us (4%)
  between operations  19.8 us (2%)
    reduce_scatter x1, waiting for transfers between devices, body(): lax.psum_scatter(jnp.dot(portion, solved_prev, preferred_element_type=jnp...  181 us
    another operation x30, other arithmetic, invert(): factor = jnp.linalg.cholesky(diagonal)  172 us
    psum x1, waiting for transfers between devices, spread(): return lax.psum(kept, axis)  115 us
    all_gather x1, waiting for transfers between devices, body(): chosen = lax.all_gather(left_factor[:block_rows], 'row', axis=0, tiled=True)  87.9 us
    another operation x3, other arithmetic, invert(): return jax.scipy.linalg.solve_triangular(factor, identity, lower=True)  83.6 us
    reduce_scatter x1, waiting for transfers between devices, body(): lax.psum_scatter(jnp.einsum('pk,mk->pm', portion, left_factor, preferred_...  57.3 us
    all_gather x1, waiting for transfers between devices, body(): diagonal = lax.all_gather(diag_part, 'col', axis=1, tiled=True)  47.7 us
    all_gather x1, blocking collectives, body(): diag_part = lax.all_gather(update[:block_rows], 'row', axis=0, tiled=True)  38.7 us
  transfers between devices with their start and end apart: 7, of which 5 were waited for; matrix products, arithmetic and copies ran while one was open for 39% of the time, Pallas kernels for 0%

commit v1 on v0

--- a/solution.py
+++ b/solution.py
@@ -6,7 +6,7 @@
 
 def spread(value, axis, source):
     kept = jnp.where(lax.axis_index(axis) == source, value, 0).astype(value.dtype)
-    return lax.psum(kept, axis)
+    return jnp.sum(lax.all_gather(kept, axis), axis=0)
 
 
 def invert(diagonal):

time: 920 us -> 729 us (0.79)
  waiting for transfers between devices: 489 us -> 280 us
    reduce_scatter x1, waiting for transfers between devices: 181 us -> 0.01 us  [body(): lax.psum_scatter(jnp.dot(portion, solved_prev, preferred_element_type=jnp...]
    psum x1 -> x0, waiting for transfers between devices: 115 us -> none  [spread(): return lax.psum(kept, axis)]
    all_gather x0 -> x1, waiting for transfers between devices: none -> 59.7 us  [spread(): return jnp.sum(lax.all_gather(kept, axis), axis=0)]
    all_gather x1, waiting for transfers between devices: 0.01 us -> 43.6 us  [body(): lax.all_gather(reduced, 'row', axis=0, tiled=True)]
    all_gather x1, waiting for transfers between devices: 47.7 us -> 31 us  [body(): diagonal = lax.all_gather(diag_part, 'col', axis=1, tiled=True)]
  transfers between devices with their start and end apart: 7 -> 7, of which waited for: 5 -> 5; matrix products, arithmetic and copies ran while one was open for 39% -> 51% of each run, Pallas kernels for 0% -> 0%
where the time goes in v1:
time: 729 us; the launch traced here: 722 us
  waiting for transfers between devices  280 us (38%)
  other arithmetic  277 us (38%)
  matrix products  68.5 us (9%)
  blocking collectives  40.7 us (6%)
  local copies, waits for them, and re-layouts  35.1 us (5%)
  between operations  19.7 us (3%)
    another operation x30, other arithmetic, invert(): factor = jnp.linalg.cholesky(diagonal)  172 us
    all_gather x1, waiting for transfers between devices, body(): chosen = lax.all_gather(left_factor[:block_rows], 'row', axis=0, tiled=True)  88 us
    another operation x3, other arithmetic, invert(): return jax.scipy.linalg.solve_triangular(factor, identity, lower=True)  84.3 us
    all_gather x1, waiting for transfers between devices, spread(): return jnp.sum(lax.all_gather(kept, axis), axis=0)  59.7 us
    reduce_scatter x1, waiting for transfers between devices, body(): lax.psum_scatter(jnp.einsum('pk,mk->pm', portion, left_factor, preferred_...  57.8 us
    all_gather x1, waiting for transfers between devices, body(): lax.all_gather(reduced, 'row', axis=0, tiled=True)  43.6 us
    all_gather x1, blocking collectives, body(): diag_part = lax.all_gather(update[:block_rows], 'row', axis=0, tiled=True)  40.7 us
    another operation x15, matrix products, invert(): return jax.scipy.linalg.solve_triangular(factor, identity, lower=True)  33.6 us
  transfers between devices with their start and end apart: 7, of which 5 were waited for; matrix products, arithmetic and copies ran while one was open for 51% of the time, Pallas kernels for 0%

profile of v1, /device:TPU:1, one launch (start us, length us, event | category | flops | bytes accessed | tf_op | source)
XLA Modules:
  0.0 721.8 jit_solution(335722015555205800)
XLA Ops:
  8.8 88.0 %all-gather.7.cloned.1.call-done = bf16[1024,1024]{1,0:T(8,128)(2,1)} async-done(((bf16[32,1024]{1,0:T(8,128)(2,1)}), bf16[1024,1024]{1,0:T(8,128)(2,1)}) %all-gather.7.cloned.1.call-update) | async-done | bytes 2097168 | tf_op jit(solution)/shard_map/all_gather | solution.py:27
  96.8 3.6 fusion.77
  101.8 57.8 %reduce-scatter.3.cloned.1.call-done = f32[64,256]{1,0:T(8,128)} async-done(((f32[1024,256]{1,0:T(8,128)}), f32[64,256]{1,0:T(8,128)}) %reduce-scatter.3.cloned.1.call-update) | async-done | bytes 65552 | tf_op jit(solution)/shard_map/reduce_scatter | solution.py:29
  160.5 40.7 %all_gather.23 = f32[1024,64]{1,0:T(8,128)S(1)} all-gather(f32[32,64]{1,0:T(8,128)S(1)} %copy.7), channel_id=1, replica_groups=mesh['row'=32,'col'=16] {'row'}, dimensions={0}, use_global_device_ids=true | all-gather | bytes 270336 | tf_op jit(solution)/shard_map/all_gather | solution.py:36
  202.2 59.7 %all-gather.15.cloned.1.call-done = bf16[16384,512]{1,0:T(8,128)(2,1)} async-done(((bf16[1024,512]{1,0:T(8,128)(2,1)}), bf16[16384,512]{1,0:T(8,128)(2,1)}) %all-gather.15.cloned.1.call-update) | async-done | bytes 16777232 | tf_op jit(solution)/shard_map/all_gather | solution.py:9
  261.9 8.9 %reduce_sum.12 = bf16[1024,512]{1,0:T(8,128)(2,1)S(1)} reduce(bf16[16,1024,512]{2,1,0:T(8,128)(2,1)} %bitcast.110, bf16[]{:T(256)} %constant.321.clone.1), dimensions={0}, to_apply=%region_17.18 | reduce | flops 7864320 | bytes 17825794 | tf_op jit(solution)/shard_map/reduce_sum | solution.py:9
  274.3 2.4 fusion.21
  276.8 31.0 %all-gather.11.cloned.1.call-done = f32[1024,1024]{0,1:T(8,128)} async-done(((f32[1024,64]{0,1:T(8,128)}), f32[1024,1024]{0,1:T(8,128)}) %all-gather.11.cloned.1.call-update) | async-done | bytes 4194320 | tf_op jit(solution)/shard_map/all_gather | solution.py:37
  307.7 5.8 copy.9
  313.6 4.4 fusion
  320.0 11.7 %cholesky.223 = f32[128,128]{1,0:T(8,128)S(1)} custom-call(f32[128,128]{1,0:T(8,128)S(1)} %cholesky.580), custom_call_target="Cholesky" | custom-call | tf_op jit(solution)/shard_map/jit(cholesky)/cholesky | solution.py:13
  331.8 9.8 %custom-call.63 = f32[1,128,128]{1,2,0:T(8,128)S(1)} custom-call(f32[1,128,128]{2,1,0:T(8,128)S(1)} %get-tuple-element.66), custom_call_target="InvertDiagBlocksLowerTriangular" | custom-call | tf_op jit(solution)/shard_map/jit(cholesky)/cholesky | solution.py:13
  341.6 2.5 cholesky.255
  344.1 2.3 constant_dynamic-update-slice_fusion.29
  348.0 11.9 %cholesky.244 = f32[128,128]{1,0:T(8,128)S(1)} custom-call(f32[128,128]{1,0:T(8,128)S(1)} %cholesky.584), custom_call_target="Cholesky" | custom-call | tf_op jit(solution)/shard_map/jit(cholesky)/cholesky | solution.py:13
  360.5 9.8 %custom-call.64 = f32[1,128,128]{1,2,0:T(8,128)S(1)} custom-call(f32[1,128,128]{2,1,0:T(8,128)S(1)} %get-tuple-element.63), custom_call_target="InvertDiagBlocksLowerTriangular" | custom-call | tf_op jit(solution)/shard_map/jit(cholesky)/cholesky | solution.py:13
  373.7 11.7 %cholesky.468 = f32[128,128]{1,0:T(8,128)S(1)} custom-call(f32[128,128]{1,0:T(8,128)S(1)} %cholesky.589), custom_call_target="Cholesky" | custom-call | tf_op jit(solution)/shard_map/jit(cholesky)/cholesky | solution.py:13
  386.7 9.8 %custom-call.65 = f32[1,128,128]{1,2,0:T(8,128)S(1)} custom-call(f32[1,128,128]{2,1,0:T(8,128)S(1)} %get-tuple-element.60), custom_call_target="InvertDiagBlocksLowerTriangular" | custom-call | tf_op jit(solution)/shard_map/jit(cholesky)/cholesky | solution.py:13
  397.7 2.3 convolution_subtract_fusion.7
  400.0 11.9 %cholesky.487 = f32[128,128]{1,0:T(8,128)S(1)} custom-call(f32[128,128]{1,0:T(8,128)S(1)} %cholesky.594), custom_call_target="Cholesky" | custom-call | tf_op jit(solution)/shard_map/jit(cholesky)/cholesky | solution.py:13
  413.2 9.8 %custom-call.66 = f32[1,128,128]{1,2,0:T(8,128)S(1)} custom-call(f32[1,128,128]{2,1,0:T(8,128)S(1)} %get-tuple-element.57), custom_call_target="InvertDiagBlocksLowerTriangular" | custom-call | tf_op jit(solution)/shard_map/jit(cholesky)/cholesky | solution.py:13
  424.1 2.4 convolution_subtract_fusion.8
  426.5 11.7 %cholesky.506 = f32[128,128]{1,0:T(8,128)S(1)} custom-call(f32[128,128]{1,0:T(8,128)S(1)} %cholesky.599), custom_call_target="Cholesky" | custom-call | tf_op jit(solution)/shard_map/jit(cholesky)/cholesky | solution.py:13
  439.6 10.2 %custom-call.67 = f32[1,128,128]{1,2,0:T(8,128)S(1)} custom-call(f32[1,128,128]{2,1,0:T(8,128)S(1)} %get-tuple-element.54), custom_call_target="InvertDiagBlocksLowerTriangular" | custom-call | tf_op jit(solution)/shard_map/jit(cholesky)/cholesky | solution.py:13
  450.7 2.3 convolution_subtract_fusion.9
  453.0 11.7 %cholesky.526 = f32[128,128]{1,0:T(8,128)S(1)} custom-call(f32[128,128]{1,0:T(8,128)S(1)} %cholesky.604), custom_call_target="Cholesky" | custom-call | tf_op jit(solution)/shard_map/jit(cholesky)/cholesky | solution.py:13
  466.0 9.8 %custom-call.68 = f32[1,128,128]{1,2,0:T(8,128)S(1)} custom-call(f32[1,128,128]{2,1,0:T(8,128)S(1)} %get-tuple-element.51), custom_call_target="InvertDiagBlocksLowerTriangular" | custom-call | tf_op jit(solution)/shard_map/jit(cholesky)/cholesky | solution.py:13
  478.9 11.9 %cholesky.546 = f32[128,128]{1,0:T(8,128)S(1)} custom-call(f32[128,128]{1,0:T(8,128)S(1)} %cholesky.609), custom_call_target="Cholesky" | custom-call | tf_op jit(solution)/shard_map/jit(cholesky)/cholesky | solution.py:13
  492.0 9.8 %custom-call.69 = f32[1,128,128]{1,2,0:T(8,128)S(1)} custom-call(f32[1,128,128]{2,1,0:T(8,128)S(1)} %get-tuple-element.48), custom_call_target="InvertDiagBlocksLowerTriangular" | custom-call | tf_op jit(solution)/shard_map/jit(cholesky)/cholesky | solution.py:13
  504.5 11.7 %cholesky.564 = f32[128,128]{1,0:T(8,128)S(1)} custom-call(f32[128,128]{1,0:T(8,128)S(1)} %convolution_subtract_fusion.11), custom_call_target="Cholesky" | custom-call | tf_op jit(solution)/shard_map/jit(cholesky)/cholesky | solution.py:13
  523.1 4.9 select_select_fusion
  528.0 22.4 %while.1 = (s32[]{:T(128)}, f32[1024,1024]{1,0:T(8,128)}, s32[8,2]{0,1:T(2,128)S(1)}, f32[8,128,128]{2,1,0:T(8,128)S(1)}, s32[]{:T(128)}) while((s32[]{:T(128)}, f32[1024,1024]{1,0:T(8,128)}, s32[8,2]{0,1:T(2,128)S(1)}, f32[8,128,128]{2,1,0:T(8,128)S(1)}, s32[]{:T(128)}) %tuple.61), condition=%wide.while_cond, body=%wide.while_body.sunk | while | flops 2 | bytes 131181 | solution.py:15
  528.6 2.2 bitcast_dynamic-update-slice_fusion.2
  531.4 2.2 bitcast_dynamic-update-slice_fusion.2
  534.2 2.2 bitcast_dynamic-update-slice_fusion.2
  537.0 2.2 bitcast_dynamic-update-slice_fusion.2
  539.8 2.2 bitcast_dynamic-update-slice_fusion.2
  542.6 2.2 bitcast_dynamic-update-slice_fusion.2
  550.3 79.4 %custom-call.70 = f32[8,128,128]{1,2,0:T(8,128)} custom-call(f32[8,128,128]{2,1,0:T(8,128)S(1)} %get-tuple-element.9), custom_call_target="InvertDiagBlocksLowerTriangular" | custom-call | tf_op jit(solution)/shard_map/jit(_solve_triangular)/triangular_solve | solution.py:15
  629.8 2.5 constant_dynamic-update-slice_fusion.17
  635.6 2.8 constant_dynamic-update-slice_fusion.16
  645.9 2.2 fusion.18
  650.0 2.6 convolution_subtract_fusion.2
  654.5 4.0 convolution_subtract_fusion.1
  659.9 3.6 convolution_subtract_fusion.3
  664.9 2.6 fusion.45
  667.6 43.6 %all-gather.13.cloned.1.call-done = f32[1024,512]{1,0:T(8,128)} async-done(((f32[32,512]{1,0:T(8,128)}), f32[1024,512]{1,0:T(8,128)}) %all-gather.13.cloned.1.call-update) | async-done | bytes 2097168 | tf_op jit(solution)/shard_map/all_gather | solution.py:62
  711.1 3.6 fusion.53
  (107 shorter events, 59.7 us)
Async XLA Ops:
  7.2 263.7 %copy-start = (bf16[512,512]{1,0:T(8,128)(2,1)S(1)}, bf16[512,512]{1,0:T(8,128)(2,1)}, u32[]{:S(2)}) copy-start(bf16[512,512]{1,0:T(8,128)(2,1)} %param.6) | copy-start | bytes 1572868
  7.2 89.6 %all-gather.7.cloned.1.call-start = ((), (), s32[]{:S(2)}) async-start(), calls=%async_computation.2 | async-start | bytes 2162688 | tf_op jit(solution)/shard_map/all_gather | solution.py:27
  8.8 150.8 %copy-start.8 = (f32[256,64]{0,1:T(8,128)S(1)}, f32[256,64]{0,1:T(8,128)}, u32[]{:S(2)}) copy-start(f32[256,64]{0,1:T(8,128)} %param.4) | copy-start | bytes 196612
  8.8 150.8 %reduce-scatter.3.cloned.1.call-start = ((), (), s32[]{:S(2)}) async-start(), calls=%async_computation.3 | async-start | bytes 1114112 | tf_op jit(solution)/shard_map/reduce_scatter | solution.py:29
  96.8 3.7 copy-start.5
  100.4 161.5 %all-gather.15.cloned.1.call-start = ((), (), s32[]{:S(2)}) async-start(), calls=%async_computation.8 | async-start | bytes 17825792 | tf_op jit(solution)/shard_map/all_gather | solution.py:9
  101.7 206.0 %all-gather.11.cloned.1.call-start = ((), (), s32[]{:S(2)}) async-start(), calls=%async_computation.5 | async-start | bytes 4456448 | tf_op jit(solution)/shard_map/all_gather | solution.py:37
  160.4 110.4 %copy-start.7 = (f32[256,64]{0,1:T(8,128)}, f32[256,64]{0,1:T(8,128)S(1)}, u32[]{:S(2)}) copy-start(f32[256,64]{0,1:T(8,128)S(1)} %bitcast_subtract_fusion) | copy-start | bytes 196612
  202.1 430.2 %reduce-scatter.5.cloned.1.call-start = ((), (), s32[]{:S(2)}) async-start(), calls=%async_computation.6 | async-start | bytes 2162688 | tf_op jit(solution)/shard_map/reduce_scatter | solution.py:52
  272.9 392.0 %all-gather.9.cloned.1.call-start = ((), (), s32[]{:S(2)}) async-start(), calls=%async_computation.4 | async-start | bytes 1114112 | tf_op jit(solution)/shard_map/all_gather | solution.py:42
  276.7 434.4 %all-gather.13.cloned.1.call-start = ((), (), s32[]{:S(2)}) async-start(), calls=%async_computation.7 | async-start | bytes 2162688 | tf_op jit(solution)/shard_map/all_gather | solution.py:62
  318.0 2.0 copy-start.3
  523.0 109.3 %copy-start.9 = (f32[32,512]{1,0:T(8,128)S(1)}, f32[32,512]{1,0:T(8,128)}, u32[]{:S(2)}) copy-start(f32[32,512]{1,0:T(8,128)} %param.7) | copy-start | bytes 196612
  633.8 4.6 copy-start.2
  633.8 6.2 copy-start.6
  654.5 4.0 copy-start.4
  659.9 54.8 %copy-start.1 = (bf16[512,512]{1,0:T(8,128)(2,1)S(1)}, bf16[512,512]{1,0:T(8,128)(2,1)}, u32[]{:S(2)}) copy-start(bf16[512,512]{1,0:T(8,128)(2,1)} %param.6) | copy-start | bytes 1572868
Sparse Core Ops, SparseCore 0:
  11.8 84.9 all-gather.6
  100.5 59.0 reduce-scatter.2
  161.9 99.9 all-gather.14
  264.1 43.5 all-gather.10
  312.6 215.5 reduce-scatter.4
  530.8 45.9 all-gather.8
  633.9 77.1 all-gather.12
